TPU v7x, 32 devices: a whole 2x2x4 slice. The times are simulated.
32 devices in a mesh: lat: 4 (over y, core), lon: 4 (over z), mesh: 2 (over x).
Axes of the slice: x: 2, y: 2, z: 4, core: 2. Of those that a mesh axis runs over, the one named last changes fastest.
Arguments:
- grid_latent: bfloat16 [32768, 512], P(('lat', 'lon', 'mesh')), may hold values from -6 to 6
- target: bfloat16 [32768, 84], P(('lat', 'lon', 'mesh')), may hold values from -6 to 6
- area: float32 [32768], P(('lat', 'lon', 'mesh')), may hold values from 0.05 to 1
- mesh_latent: bfloat16 [10240, 512], P(('lat', 'lon', 'mesh')), may hold values from -6 to 6
- node_gain: float32 [512], replicated, may hold values from 0.1 to 1.9
- w_enc: bfloat16 [512, 512], replicated, may hold values from -0.25 to 0.25
- w_up: bfloat16 [512, 512], replicated, may hold values from -0.25 to 0.25
- w_down: bfloat16 [512, 512], replicated, may hold values from -0.25 to 0.25
- w_msg: bfloat16 [512, 512], replicated, may hold values from -0.25 to 0.25
- w_dec: bfloat16 [512, 512], replicated, may hold values from -0.25 to 0.25
- w_out: bfloat16 [512, 84], replicated, may hold values from -0.25 to 0.25
- enc_cell: int32 [32, 3, 3, 2, 85], P(('lat', 'lon', 'mesh')), may hold values from 0 to 1023
- enc_live: int32 [32, 3, 3, 2], P(('lat', 'lon', 'mesh')), may hold values from 1 to 85, as said below
- enc_weight: float32 [32, 3, 3, 2, 85], P(('lat', 'lon', 'mesh')), may hold values from 0.2 to 1
- enc_node: int32 [32, 3, 3, 2, 85], P(('lat', 'lon', 'mesh')), may hold values from 0 to 319
- dec_node: int32 [32, 3, 3, 2, 128], P(('lat', 'lon', 'mesh')), may hold values from 0 to 319
- dec_cell: int32 [32, 3, 3, 2, 128], P(('lat', 'lon', 'mesh')), may hold values from 0 to 1023
- dec_weight: float32 [32, 3, 3, 2, 128], P(('lat', 'lon', 'mesh')), may hold values from 0.2 to 1
Outputs:
- grid_grad: float32 [32768, 512], P(('lat', 'lon', 'mesh'))
- grad_enc: float32 [512, 512], P(('lat', 'lon', 'mesh'))
- grad_up: float32 [512, 512], P(('lat', 'lon', 'mesh'))
- grad_down: float32 [512, 512], P(('lat', 'lon', 'mesh'))
- grad_msg: float32 [512, 512], P(('lat', 'lon', 'mesh'))
- grad_dec: float32 [512, 512], P(('lat', 'lon', 'mesh'))
- grad_out: float32 [512, 84], P(('lat', 'lon', 'mesh'))
Inputs may be any that keep to these rules, and one draw needn't show every extreme that they name: Slots 0 to enc_live - 1 of a bucket are edges, the others padding; in every draw some mesh owner receives 85 live slots in every bucket addressed to it. `enc_cell`: local cell indices. `enc_node`: local node indices. `dec_node`: local node indices. `dec_cell`: local cell indices.
All inputs are finite; a program needn't handle non-finite values.
Results may differ from a plain program's by a relative error of at most 0.0085.
Values may be sent and summed in bfloat16 or wider, within the bound.
No kernel may reach another device: no remote copies, remote signals or barrier semaphores. Data moves between devices by JAX's collectives and lax.ppermute only.
A program may use at most 128 MiB of HBM per device.

v0:
```python
import jax
import jax.numpy as jnp
from jax import lax
from jax.sharding import PartitionSpec as P


def extended_2(cells, sides, width):
    for axis, dim in sides:
        count = lax.axis_size(axis)
        head = lax.slice_in_dim(cells, 0, width, axis=dim)
        tail = lax.slice_in_dim(cells, cells.shape[dim] - width, cells.shape[dim], axis=dim)
        cells = jnp.concatenate(
            [
                lax.ppermute(tail, axis, [(i, (i + 1) % count) for i in range(count)]),
                cells,
                lax.ppermute(head, axis, [((i + 1) % count, i) for i in range(count)]),
            ],
            axis=dim,
        )
    return cells


def matmul(left, right):
    return jnp.dot(left, right, preferred_element_type=jnp.float32)


def contract(left, right):
    return lax.dot_general(
        left, right, (((0,), (0,)), ((), ())), preferred_element_type=jnp.float32
    )


def silu_slope(argument):
    sigmoid_value = jax.nn.sigmoid(argument)
    return sigmoid_value * (1.0 + argument * (1.0 - sigmoid_value))


def node_forward(node_state, node_gain, w_up, w_down):
    inv_rms = lax.rsqrt(jnp.mean(node_state * node_state, axis=-1, keepdims=True) + 1e-05)
    normed = (node_state * inv_rms * node_gain).astype(jnp.bfloat16)
    activation = matmul(normed, w_up)
    hidden = jax.nn.silu(activation).astype(jnp.bfloat16)
    updated = node_state + matmul(hidden, w_down)
    return (updated, inv_rms, normed, activation, hidden)


def node_backward(
    back_node, node_state, node_gain, w_up, w_down, inv_rms, normed, activation, hidden
):
    back_node_half = back_node.astype(jnp.bfloat16)
    grad_down = contract(hidden, back_node_half)
    back_hidden = matmul(back_node_half, w_down.T)
    back_act = (back_hidden * silu_slope(activation)).astype(jnp.bfloat16)
    grad_up = contract(normed, back_act)
    back_norm = matmul(back_act, w_up.T) * node_gain
    mean_term = jnp.mean(node_state * back_norm, axis=-1, keepdims=True)
    back_state = back_node + inv_rms * back_norm - node_state * inv_rms**3 * mean_term
    return (back_state, grad_up, grad_down)


def route_enc(bucket):
    crossed = lax.all_to_all(bucket, "mesh", split_axis=2, concat_axis=2, tiled=True)
    extended = extended_2(crossed, (("lat", 0), ("lon", 1)), 1)
    result = extended[::-2, ::-2]
    return result


def route_dec(bucket):
    crossed = lax.all_to_all(bucket, "mesh", split_axis=2, concat_axis=2, tiled=True)
    extended = extended_2(crossed, (("lat", 0), ("lon", 1)), 1)
    result = extended[::-2, ::-2]
    return result


def on_device(
    grid_latent,
    target,
    area,
    mesh_latent,
    node_gain,
    w_enc,
    w_up,
    w_down,
    w_msg,
    w_dec,
    w_out,
    enc_cell,
    enc_live,
    enc_weight,
    enc_node,
    dec_node,
    dec_cell,
    dec_weight,
):
    cell_rows = grid_latent.shape[0]
    node_rows = mesh_latent.shape[0]
    features = grid_latent.shape[1]
    send_cells = enc_cell[0]
    offsets = jnp.arange(3, dtype=jnp.int32) - 1
    lat_here = lax.axis_index("lat")
    lat_count = lax.axis_size("lat")
    reach_up = lat_here + offsets
    send_ok = (reach_up >= 0) & (reach_up < lat_count)
    reach_down = lat_here - offsets
    recv_ok = (reach_down >= 0) & (reach_down < lat_count)
    slot_index = jnp.arange(send_cells.shape[-1], dtype=jnp.int32)
    edge_scale = jnp.where(
        (slot_index < enc_live[0][..., None]) & send_ok[:, None, None, None],
        enc_weight[0],
        jnp.float32(0.0),
    )
    dec_scale = jnp.where(recv_ok[:, None, None, None], dec_weight[0], jnp.float32(0.0))
    projected = matmul(grid_latent, w_enc).astype(jnp.bfloat16)
    outgoing = (edge_scale[..., None] * projected[send_cells].astype(jnp.float32)).astype(
        jnp.bfloat16
    )
    landed = route_enc(outgoing)
    aggregate = jax.ops.segment_sum(
        landed.reshape(-1, features).astype(jnp.float32),
        enc_node[0].reshape(-1),
        num_segments=node_rows,
    )
    node_state = mesh_latent.astype(jnp.float32) + aggregate
    updated, inv_rms, normed, activation, hidden = node_forward(node_state, node_gain, w_up, w_down)
    node_half = updated.astype(jnp.bfloat16)
    leaving = node_half[dec_node[0]]
    pulled = route_dec(leaving)
    row_block = pulled.reshape(-1, features)
    preact = matmul(row_block, w_msg)
    edge_weight = dec_scale.reshape(-1)[:, None]
    cell_ids = dec_cell[0].reshape(-1)
    weighted = edge_weight * jax.nn.silu(preact)
    gathered = jax.ops.segment_sum(weighted, cell_ids, num_segments=cell_rows).astype(jnp.bfloat16)
    blended = grid_latent.astype(jnp.float32) + matmul(gathered, w_dec)
    blended_half = blended.astype(jnp.bfloat16)
    output = matmul(blended_half, w_out)
    residual = (area[:, None] * (output - target.astype(jnp.float32))).astype(jnp.bfloat16)
    grad_out = contract(blended_half, residual) / cell_rows
    back_blend = matmul(residual, w_out.T)
    back_half = back_blend.astype(jnp.bfloat16)
    grad_dec = contract(gathered, back_half) / cell_rows
    back_gather = matmul(back_half, w_dec.T).astype(jnp.bfloat16)
    back_message = edge_weight * back_gather[cell_ids].astype(jnp.float32)
    back_preact = (back_message * silu_slope(preact)).astype(jnp.bfloat16)
    grad_msg = contract(row_block, back_preact) / cell_rows
    back_pulled = matmul(back_preact, w_msg.T).astype(jnp.bfloat16).reshape(pulled.shape)
    returned = route_dec(back_pulled[::-1, ::-1])[::-1, ::-1]
    back_node = jax.ops.segment_sum(
        returned.reshape(-1, features).astype(jnp.float32),
        dec_node[0].reshape(-1),
        num_segments=node_rows,
    )
    back_state, grad_up, grad_down = node_backward(
        back_node, node_state, node_gain, w_up, w_down, inv_rms, normed, activation, hidden
    )
    back_state_half = back_state.astype(jnp.bfloat16)
    toward = back_state_half[enc_node[0]]
    came_back = route_enc(toward[::-1, ::-1])[::-1, ::-1]
    weighted_back = (edge_scale[..., None] * came_back.astype(jnp.float32)).reshape(-1, features)
    back_proj = jax.ops.segment_sum(
        weighted_back, send_cells.reshape(-1), num_segments=cell_rows
    ).astype(jnp.bfloat16)
    grad_enc = contract(grid_latent, back_proj) / cell_rows
    grid_grad = back_blend + matmul(back_proj, w_enc.T)
    partials = (grad_enc, grad_up / cell_rows, grad_down / cell_rows, grad_msg, grad_dec, grad_out)
    totals = lax.psum(
        (partials[0], partials[1], partials[2], partials[3], partials[4], partials[5]),
        ("lat", "lon", "mesh"),
    )
    row_share = features // lax.axis_size(("lat", "lon", "mesh"))
    row_start = lax.axis_index(("lat", "lon", "mesh")) * row_share
    shares = tuple((lax.dynamic_slice_in_dim(total, row_start, row_share, 0) for total in totals))
    return (grid_grad,) + tuple(shares)


def solution(mesh):
    placed = (
        P(("lat", "lon", "mesh"), None),
        P(("lat", "lon", "mesh"), None),
        P(("lat", "lon", "mesh")),
        P(("lat", "lon", "mesh"), None),
        P(),
        P(),
        P(),
        P(),
        P(),
        P(),
        P(),
        P(("lat", "lon", "mesh"), None, None, None, None),
        P(("lat", "lon", "mesh"), None, None, None),
        P(("lat", "lon", "mesh"), None, None, None, None),
        P(("lat", "lon", "mesh"), None, None, None, None),
        P(("lat", "lon", "mesh"), None, None, None, None),
        P(("lat", "lon", "mesh"), None, None, None, None),
        P(("lat", "lon", "mesh"), None, None, None, None),
    )
    return jax.shard_map(
        on_device,
        mesh=mesh,
        in_specs=placed,
        out_specs=(
            P(("lat", "lon", "mesh"), None),
            P(("lat", "lon", "mesh"), None),
            P(("lat", "lon", "mesh"), None),
            P(("lat", "lon", "mesh"), None),
            P(("lat", "lon", "mesh"), None),
            P(("lat", "lon", "mesh"), None),
            P(("lat", "lon", "mesh"), None),
        ),
        check_vma=False,
    )
```

profile of v0, /device:TPU:0, one launch (start us, length us, event | category | flops | bytes accessed | tf_op | source)
XLA Modules:
  0.0 727.9 jit_solution(15352589680667660315)
XLA Ops:
  10.2 2.1 convolution_convert_fusion.2
  12.3 4.8 gather_fusion
  17.1 2.1 reshape.272
  20.0 2.2 multiply_convert_fusion.1
  22.3 23.8 %all_to_all.20 = bf16[3,3,2,85,512]{4,3,1,0,2:T(8,128)(2,1)S(1)} all-to-all(bf16[3,3,2,85,512]{4,3,1,0,2:T(8,128)(2,1)S(1)} %copy.55), channel_id=1, replica_groups=mesh['lat'=4,'lon'=4,'mesh'=2] {'mesh'}, dimensions={2} | all-to-all | bytes 3133440 | tf_op jit(solution)/shard_map/all_to_all | solution.py:62
  48.8 9.5 %collective-permute-done = bf16[1,3,2,85,512]{4,2,3,1,0:T(2,128)(2,1)S(1)} collective-permute-done((bf16[1,3,2,85,512]{4,2,3,1,0:T(2,128)(2,1)S(1)}, bf16[1,3,2,85,512]{4,2,3,1,0:T(2,128)(2,1)S(1)}, u32[]{:S(2)}, u32[]{:S(2)}) %collective-permute-start) | collective-permute-done | bytes 522272 | tf_op jit(solution)/shard_map/ppermute | solution.py:14
  61.0 3.7 collective-permute-start.3
  67.2 17.3 %collective-permute-done.3 = bf16[5,1,2,85,512]{4,2,3,1,0:T(2,128)(2,1)S(1)} collective-permute-done((bf16[5,1,2,85,512]{4,2,3,1,0:T(2,128)(2,1)S(1)}, bf16[5,1,2,85,512]{4,2,3,1,0:T(2,128)(2,1)S(1)}, u32[]{:S(2)}, u32[]{:S(2)}) %collective-permute-start.3) | collective-permute-done | bytes 870432 | tf_op jit(solution)/shard_map/ppermute | solution.py:16
  84.6 19.3 %collective-permute-done.2 = bf16[5,1,2,85,512]{4,2,3,1,0:T(2,128)(2,1)} collective-permute-done((bf16[5,1,2,85,512]{4,2,3,1,0:T(2,128)(2,1)}, bf16[5,1,2,85,512]{4,2,3,1,0:T(2,128)(2,1)}, u32[]{:S(2)}, u32[]{:S(2)}) %collective-permute-start.2) | collective-permute-done | bytes 870432 | tf_op jit(solution)/shard_map/ppermute | solution.py:14
  106.4 2.0 copy.64
  108.4 3.6 reshape.237
  112.0 10.6 %scatter_fusion = f32[320,512]{1,0:T(8,128)S(1)} fusion(f32[320,512]{1,0:T(8,128)S(1)} %convert_element_type.79, s32[1530]{0:T(1024)S(1)} %reshape.235, f32[1530,512]{1,0:T(8,128)} %reshape.237), kind=kCustom, calls=%fused_computation.4 | custom fusion | flops 783360 | bytes 9406440 | tf_op jit(solution)/shard_map/scatter-add | solution.py:118
  125.0 7.5 %gather_fusion.1 = bf16[2304,512]{1,0:T(8,128)(2,1)} fusion(bf16[320,512]{1,0:T(8,128)(2,1)S(1)} %fusion.6, s32[3072]{0:T(1024)S(1)} %get-tuple-element.62), kind=kCustom, calls=%fused_computation.1 | custom fusion | bytes 4727808 | tf_op jit(solution)/shard_map/gather | solution.py:126
  134.3 30.6 %all_to_all.21 = bf16[3,3,2,128,512]{4,3,1,0,2:T(8,128)(2,1)S(1)} all-to-all(bf16[3,3,2,128,512]{4,3,1,0,2:T(8,128)(2,1)S(1)} %copy.65), channel_id=1, replica_groups=mesh['lat'=4,'lon'=4,'mesh'=2] {'mesh'}, dimensions={2} | all-to-all | bytes 4718592 | tf_op jit(solution)/shard_map/all_to_all | solution.py:69
  165.3 2.3 collective-permute-start.5
  167.6 14.9 %collective-permute-done.4 = bf16[1,3,2,128,512]{4,3,2,1,0:T(8,128)(2,1)S(1)} collective-permute-done((bf16[1,3,2,128,512]{4,3,2,1,0:T(8,128)(2,1)S(1)}, bf16[1,3,2,128,512]{4,3,2,1,0:T(8,128)(2,1)S(1)}, u32[]{:S(2)}, u32[]{:S(2)}) %collective-permute-start.4) | collective-permute-done | bytes 786464 | tf_op jit(solution)/shard_map/ppermute | solution.py:14
  189.5 2.2 collective-permute-start.7
  192.5 29.1 %collective-permute-done.6 = bf16[5,1,2,128,512]{4,3,2,1,0:T(8,128)(2,1)S(1)} collective-permute-done((bf16[5,1,2,128,512]{4,3,2,1,0:T(8,128)(2,1)}, bf16[5,1,2,128,512]{4,3,2,1,0:T(8,128)(2,1)S(1)}, u32[]{:S(2)}, u32[]{:S(2)}) %collective-permute-start.6) | collective-permute-done | bytes 1310752 | tf_op jit(solution)/shard_map/ppermute | solution.py:14
  221.6 27.4 %collective-permute-done.7 = bf16[5,1,2,128,512]{4,3,2,1,0:T(8,128)(2,1)} collective-permute-done((bf16[5,1,2,128,512]{4,3,2,1,0:T(8,128)(2,1)}, bf16[5,1,2,128,512]{4,3,2,1,0:T(8,128)(2,1)}, u32[]{:S(2)}, u32[]{:S(2)}) %collective-permute-start.7) | collective-permute-done | bytes 1310752 | tf_op jit(solution)/shard_map/ppermute | solution.py:16
  249.0 3.3 pad_maximum_fusion
  257.2 3.5 fusion.33
  260.7 22.0 %scatter_custom_fusion.1 = f32[1024,512]{1,0:T(8,128)S(1)} fusion(s32[2304]{0:T(1024)} %reshape.243, f32[2304,512]{1,0:T(8,128)} %fusion.33, f32[]{:T(128)} %constant.24.clone.1, f32[2304]{0:T(1024)S(1)} %broadcast_select_fusion, f32[]{:T(128)} %constant.16.clone.1), kind=kCustom, calls=%fused_computation.11 | custom fusion | flops 7077888 | bytes 6825984 | tf_op jit(solution)/shard_map/scatter-add | solution.py:133
  282.7 2.9 add_convert_fusion
  290.3 7.5 %gather_fusion.2 = bf16[2304,512]{1,0:T(8,128)(2,1)} fusion(bf16[1024,512]{1,0:T(8,128)(2,1)S(1)} %convolution_convert_fusion.1, s32[3072]{0:T(1024)S(1)} %copy-done.31), kind=kCustom, calls=%fused_computation.2 | custom fusion | bytes 4727808 | tf_op jit(solution)/shard_map/gather | solution.py:143
  297.9 4.1 multiply_convert_fusion
  305.3 31.4 %all_to_all.22 = bf16[3,3,2,128,512]{4,3,1,0,2:T(8,128)(2,1)S(1)} all-to-all(bf16[3,3,2,128,512]{4,3,1,0,2:T(8,128)(2,1)} %rev.18), channel_id=1, replica_groups=mesh['lat'=4,'lon'=4,'mesh'=2] {'mesh'}, dimensions={2} | all-to-all | bytes 4718592 | tf_op jit(solution)/shard_map/all_to_all | solution.py:69
  338.6 16.0 %collective-permute-done.8 = bf16[1,3,2,128,512]{4,3,1,0,2:T(8,128)(2,1)S(1)} collective-permute-done((bf16[1,3,2,128,512]{4,3,1,0,2:T(8,128)(2,1)S(1)}, bf16[1,3,2,128,512]{4,3,1,0,2:T(8,128)(2,1)S(1)}, u32[]{:S(2)}, u32[]{:S(2)}) %collective-permute-start.8) | collective-permute-done | bytes 786464 | tf_op jit(solution)/shard_map/ppermute | solution.py:14
  356.2 2.0 copy-done.6
  361.1 2.5 collective-permute-start.11
  363.6 29.9 %collective-permute-done.10 = bf16[5,1,2,128,512]{4,3,1,0,2:T(8,128)(2,1)S(1)} collective-permute-done((bf16[5,1,2,128,512]{4,3,1,0,2:T(8,128)(2,1)}, bf16[5,1,2,128,512]{4,3,1,0,2:T(8,128)(2,1)S(1)}, u32[]{:S(2)}, u32[]{:S(2)}) %collective-permute-start.10) | collective-permute-done | bytes 1310752 | tf_op jit(solution)/shard_map/ppermute | solution.py:14
  393.5 27.1 %collective-permute-done.11 = bf16[5,1,2,128,512]{4,3,1,0,2:T(8,128)(2,1)} collective-permute-done((bf16[5,1,2,128,512]{4,3,1,0,2:T(8,128)(2,1)}, bf16[5,1,2,128,512]{4,3,1,0,2:T(8,128)(2,1)}, u32[]{:S(2)}, u32[]{:S(2)}) %collective-permute-start.11) | collective-permute-done | bytes 1310752 | tf_op jit(solution)/shard_map/ppermute | solution.py:16
  420.6 3.3 pad_maximum_fusion.1
  424.5 2.9 copy.70
  427.5 16.6 %scatter_custom_fusion.2 = f32[320,512]{1,0:T(8,128)S(1)} fusion(s32[2304]{0:T(1024)S(1)} %reshape.251, f32[2304,512]{1,0:T(8,128)} %bitcast.57, f32[]{:T(128)} %constant.16.clone.1), kind=kCustom, calls=%fused_computation.63 | custom fusion | flops 1179648 | bytes 655872 | tf_op jit(solution)/shard_map/scatter-add | solution.py:148
  446.9 4.8 gather_fusion.3
  456.4 4.6 all-to-all-start.3
  461.8 19.0 %all-to-all-done.3 = bf16[3,3,2,85,512]{4,3,1,0,2:T(8,128)(2,1)} async-done(((bf16[3,3,2,85,512]{4,3,1,0,2:T(8,128)(2,1)}), bf16[3,3,2,85,512]{4,3,1,0,2:T(8,128)(2,1)}, u32[]{:S(2)}, u32[]{:S(2)}) %all-to-all-start.3) | async-done | bytes 1566752 | tf_op jit(solution)/shard_map/all_to_all | solution.py:62
  482.8 2.4 convolution_multiply_fusion.7
  485.2 2.4 convolution_multiply_fusion.1
  493.0 3.5 collective-permute-done.13
  498.1 2.4 collective-permute-start.15
  505.6 14.1 %collective-permute-done.15 = bf16[5,1,2,85,512]{4,2,3,1,0:T(2,128)(2,1)S(1)} collective-permute-done((bf16[5,1,2,85,512]{4,2,3,1,0:T(2,128)(2,1)S(1)}, bf16[5,1,2,85,512]{4,2,3,1,0:T(2,128)(2,1)S(1)}, u32[]{:S(2)}, u32[]{:S(2)}) %collective-permute-start.15) | collective-permute-done | bytes 870432 | tf_op jit(solution)/shard_map/ppermute | solution.py:16
  519.9 19.1 %collective-permute-done.14 = bf16[5,1,2,85,512]{4,2,3,1,0:T(2,128)(2,1)S(1)} collective-permute-done((bf16[5,1,2,85,512]{4,2,3,1,0:T(2,128)(2,1)S(1)}, bf16[5,1,2,85,512]{4,2,3,1,0:T(2,128)(2,1)S(1)}, u32[]{:S(2)}, u32[]{:S(2)}) %collective-permute-start.14) | collective-permute-done | bytes 870432 | tf_op jit(solution)/shard_map/ppermute | solution.py:14
  541.8 3.7 reshape.261
  545.5 11.6 %scatter_custom_fusion.3 = f32[1024,512]{1,0:T(8,128)} fusion(s32[1530]{0:T(1024)} %reshape.259, f32[1530,512]{1,0:T(8,128)} %reshape.261, f32[]{:T(128)} %constant.16.clone.1), kind=kCustom, calls=%fused_computation.44 | custom fusion | flops 783360 | bytes 2097664 | tf_op jit(solution)/shard_map/scatter-add | solution.py:160
  557.1 3.6 fusion.5
  561.7 3.7 convolution_add_fusion
  565.4 146.7 %all-reduce.3.cloned.1.call-done = (f32[512,512]{0,1:T(8,128)}, f32[512,512]{1,0:T(8,128)}, f32[512,512]{1,0:T(8,128)}, f32[512,512]{1,0:T(8,128)}, f32[512,512]{1,0:T(8,128)}, /*index=5*/f32[512,84]{1,0:T(8,128)}) async-done(((f32[512,512]{0,1:T(8,128)}, f32[512,512]{1,0:T(8,128)}, f32[512,512]{1,0:T(8,128)}, f32[512,512]{1,0:T(8,128)}, f32[512,512]{1,0:T(8,128)}, /*index=5*/f32[512,84]{1,0:T(8,128)}), ...) | async-done | bytes 5414928 | tf_op jit(solution)/shard_map/psum | solution.py:166
  (200 shorter events, 81.0 us)
Async XLA Ops:
  7.2 250.0 %copy-start = (bf16[512,512]{1,0:T(8,128)(2,1)S(1)}, bf16[512,512]{1,0:T(8,128)(2,1)}, u32[]{:S(2)}) copy-start(bf16[512,512]{1,0:T(8,128)(2,1)} %param.26) | copy-start | bytes 1572868
  46.6 11.7 %collective-permute-start = (bf16[1,3,2,85,512]{4,2,3,1,0:T(2,128)(2,1)S(1)}, bf16[1,3,2,85,512]{4,2,3,1,0:T(2,128)(2,1)S(1)}, u32[]{:S(2)}, u32[]{:S(2)}) collective-permute-start(bf16[1,3,2,85,512]{4,2,3,1,0:T(2,128)(2,1)S(1)} %copy.56), channel_id=1, source_target_pairs={{0,8},{8,16},{16,24},{24,0},{1,9},{9,17},{17,25},{25,1},{2,10},{10... | collective-permute-start | bytes 1566728 | tf_op jit(solution)/shard_map/ppermute | solution.py:14
  47.0 13.0 %collective-permute-start.1 = (bf16[1,3,2,85,512]{4,2,3,1,0:T(2,128)(2,1)S(1)}, bf16[1,3,2,85,512]{4,2,3,1,0:T(2,128)(2,1)S(1)}, u32[]{:S(2)}, u32[]{:S(2)}) collective-permute-start(bf16[1,3,2,85,512]{4,2,3,1,0:T(2,128)(2,1)S(1)} %copy.57), channel_id=1, source_target_pairs={{8,0},{16,8},{24,16},{0,24},{9,1},{17,9},{25,17},{1,25},{10,2},{18... | collective-permute-start | bytes 1566728 | tf_op jit(solution)/shard_map/ppermute | solution.py:16
  60.1 6.2 copy-start.10
  60.1 6.1 copy-start.33
  60.1 6.2 copy-start.35
  60.2 6.3 copy-start.27
  60.3 6.2 copy-start.37
  61.0 23.4 %collective-permute-start.3 = (bf16[5,1,2,85,512]{4,2,3,1,0:T(2,128)(2,1)S(1)}, bf16[5,1,2,85,512]{4,2,3,1,0:T(2,128)(2,1)S(1)}, u32[]{:S(2)}, u32[]{:S(2)}) collective-permute-start(bf16[5,1,2,85,512]{4,2,3,1,0:T(2,128)(2,1)S(1)} %copy.61), channel_id=1, source_target_pairs={{2,0},{4,2},{6,4},{0,6},{3,1},{5,3},{7,5},{1,7},{10,8},{12,10},{14... | collective-permute-start | bytes 2611208 | tf_op jit(solution)/shard_map/ppermute | solution.py:16
  66.3 37.6 %collective-permute-start.2 = (bf16[5,1,2,85,512]{4,2,3,1,0:T(2,128)(2,1)}, bf16[5,1,2,85,512]{4,2,3,1,0:T(2,128)(2,1)}, u32[]{:S(2)}, u32[]{:S(2)}) collective-permute-start(bf16[5,1,2,85,512]{4,2,3,1,0:T(2,128)(2,1)} %copy.60), channel_id=1, source_target_pairs={{0,2},{2,4},{4,6},{6,0},{1,3},{3,5},{5,7},{7,1},{8,10},{10,12},{12... | collective-permute-start | bytes 2611208 | tf_op jit(solution)/shard_map/ppermute | solution.py:14
  66.4 38.8 %copy-start.11 = (bf16[5,3,2,85,512]{4,3,1,0,2:T(8,128)(2,1)S(1)}, bf16[5,3,2,85,512]{4,3,1,0,2:T(8,128)(2,1)}, u32[]{:S(2)}) copy-start(bf16[5,3,2,85,512]{4,3,1,0,2:T(8,128)(2,1)} %copy-done.10) | copy-start | bytes 7833604
  112.0 11.4 %copy-start.17 = (bf16[512,512]{1,0:T(8,128)(2,1)S(1)}, bf16[512,512]{1,0:T(8,128)(2,1)}, u32[]{:S(2)}) copy-start(bf16[512,512]{1,0:T(8,128)(2,1)} %param.24) | copy-start | bytes 1572868
  112.0 11.4 %copy-start.38 = (f32[512]{0:T(512)S(1)}, f32[512]{0:T(512)}, u32[]{:S(2)}) copy-start(f32[512]{0:T(512)} %param.22) | copy-start | bytes 6148
  112.0 12.6 %copy-start.45 = (bf16[512,512]{1,0:T(8,128)(2,1)S(1)}, bf16[512,512]{1,0:T(8,128)(2,1)}, u32[]{:S(2)}) copy-start(bf16[512,512]{1,0:T(8,128)(2,1)} %param.25) | copy-start | bytes 1572868
  165.2 17.3 %collective-permute-start.4 = (bf16[1,3,2,128,512]{4,3,2,1,0:T(8,128)(2,1)S(1)}, bf16[1,3,2,128,512]{4,3,2,1,0:T(8,128)(2,1)S(1)}, u32[]{:S(2)}, u32[]{:S(2)}) collective-permute-start(bf16[1,3,2,128,512]{4,3,2,1,0:T(8,128)(2,1)S(1)} %copy.96), channel_id=1, source_target_pairs={{0,8},{8,16},{16,24},{24,0},{1,9},{9,17},{17,25},{25,1},{2,10},{10... | collective-permute-start | bytes 2359304 | tf_op jit(solution)/shard_map/ppermute | solution.py:14
  165.3 18.9 %collective-permute-start.5 = (bf16[1,3,2,128,512]{4,3,2,1,0:T(8,128)(2,1)S(1)}, bf16[1,3,2,128,512]{4,3,2,1,0:T(8,128)(2,1)S(1)}, u32[]{:S(2)}, u32[]{:S(2)}) collective-permute-start(bf16[1,3,2,128,512]{4,3,2,1,0:T(8,128)(2,1)S(1)} %copy.97), channel_id=1, source_target_pairs={{8,0},{16,8},{24,16},{0,24},{9,1},{17,9},{25,17},{1,25},{10,2},{18... | collective-permute-start | bytes 2359304 | tf_op jit(solution)/shard_map/ppermute | solution.py:16
  186.2 6.2 copy-start.42
  187.9 33.7 %collective-permute-start.6 = (bf16[5,1,2,128,512]{4,3,2,1,0:T(8,128)(2,1)}, bf16[5,1,2,128,512]{4,3,2,1,0:T(8,128)(2,1)S(1)}, u32[]{:S(2)}, u32[]{:S(2)}) collective-permute-start(bf16[5,1,2,128,512]{4,3,2,1,0:T(8,128)(2,1)} %get-tuple-element.43), channel_id=1, source_target_pairs={{0,2},{2,4},{4,6},{6,0},{1,3},{3,5},{5,7},{7,1},{8,10},{10,12},{12... | collective-permute-start | bytes 3932168 | tf_op jit(solution)/shard_map/ppermute | solution.py:14
  189.5 59.5 %collective-permute-start.7 = (bf16[5,1,2,128,512]{4,3,2,1,0:T(8,128)(2,1)}, bf16[5,1,2,128,512]{4,3,2,1,0:T(8,128)(2,1)}, u32[]{:S(2)}, u32[]{:S(2)}) collective-permute-start(bf16[5,1,2,128,512]{4,3,2,1,0:T(8,128)(2,1)} %get-tuple-element.44), channel_id=1, source_target_pairs={{2,0},{4,2},{6,4},{0,6},{3,1},{5,3},{7,5},{1,7},{10,8},{12,10},{14... | collective-permute-start | bytes 3932168 | tf_op jit(solution)/shard_map/ppermute | solution.py:16
  282.7 4.4 copy-start.3
  282.7 3.9 copy-start.26
  282.7 3.9 copy-start.28
  282.7 3.9 copy-start.44
  286.7 2.9 copy-start.16
  287.8 2.5 copy-start.31
  336.8 17.8 %collective-permute-start.8 = (bf16[1,3,2,128,512]{4,3,1,0,2:T(8,128)(2,1)S(1)}, bf16[1,3,2,128,512]{4,3,1,0,2:T(8,128)(2,1)S(1)}, u32[]{:S(2)}, u32[]{:S(2)}) collective-permute-start(bf16[1,3,2,128,512]{4,3,1,0,2:T(8,128)(2,1)S(1)} %get-tuple-element.50), channel_id=1, source_target_pairs={{0,8},{8,16},{16,24},{24,0},{1,9},{9,17},{17,25},{25,1},{2,10},{10... | collective-permute-start | bytes 2359304 | tf_op jit(solution)/shard_map/ppermute | solution.py:14
  336.9 19.2 %collective-permute-start.9 = (bf16[1,3,2,128,512]{4,3,1,0,2:T(8,128)(2,1)S(1)}, bf16[1,3,2,128,512]{4,3,1,0,2:T(8,128)(2,1)S(1)}, u32[]{:S(2)}, u32[]{:S(2)}) collective-permute-start(bf16[1,3,2,128,512]{4,3,1,0,2:T(8,128)(2,1)S(1)} %get-tuple-element.49), channel_id=1, source_target_pairs={{8,0},{16,8},{24,16},{0,24},{9,1},{17,9},{25,17},{1,25},{10,2},{18... | collective-permute-start | bytes 2359304 | tf_op jit(solution)/shard_map/ppermute | solution.py:16
  358.2 5.5 copy-start.36
  359.8 33.7 %collective-permute-start.10 = (bf16[5,1,2,128,512]{4,3,1,0,2:T(8,128)(2,1)}, bf16[5,1,2,128,512]{4,3,1,0,2:T(8,128)(2,1)S(1)}, u32[]{:S(2)}, u32[]{:S(2)}) collective-permute-start(bf16[5,1,2,128,512]{4,3,1,0,2:T(8,128)(2,1)} %get-tuple-element.41), channel_id=1, source_target_pairs={{0,2},{2,4},{4,6},{6,0},{1,3},{3,5},{5,7},{7,1},{8,10},{10,12},{12... | collective-permute-start | bytes 3932168 | tf_op jit(solution)/shard_map/ppermute | solution.py:14
  361.1 59.5 %collective-permute-start.11 = (bf16[5,1,2,128,512]{4,3,1,0,2:T(8,128)(2,1)}, bf16[5,1,2,128,512]{4,3,1,0,2:T(8,128)(2,1)}, u32[]{:S(2)}, u32[]{:S(2)}) collective-permute-start(bf16[5,1,2,128,512]{4,3,1,0,2:T(8,128)(2,1)} %get-tuple-element.42), channel_id=1, source_target_pairs={{2,0},{4,2},{6,4},{0,6},{3,1},{5,3},{7,5},{1,7},{10,8},{12,10},{14... | collective-permute-start | bytes 3932168 | tf_op jit(solution)/shard_map/ppermute | solution.py:16
  424.5 19.6 %copy-start.23 = (f32[320,512]{1,0:T(8,128)S(1)}, f32[320,512]{1,0:T(8,128)}, u32[]{:S(2)}) copy-start(f32[320,512]{1,0:T(8,128)} %copy-done.22) | copy-start | bytes 1966084
  427.5 18.4 %copy-start.18 = (bf16[512,512]{1,0:T(8,128)(2,1)S(1)}, bf16[512,512]{1,0:T(8,128)(2,1)}, u32[]{:S(2)}) copy-start(bf16[512,512]{1,0:T(8,128)(2,1)} %param.24) | copy-start | bytes 1572868
  427.5 18.4 %copy-start.39 = (f32[512]{0:T(512)S(1)}, f32[512]{0:T(512)}, u32[]{:S(2)}) copy-start(f32[512]{0:T(512)} %param.22) | copy-start | bytes 6148
  455.1 6.1 copy-start.34
  456.4 24.4 %all-to-all-start.3 = ((bf16[3,3,2,85,512]{4,3,1,0,2:T(8,128)(2,1)}), bf16[3,3,2,85,512]{4,3,1,0,2:T(8,128)(2,1)}, u32[]{:S(2)}, u32[]{:S(2)}) async-start(bf16[3,3,2,85,512]{4,3,1,0,2:T(8,128)(2,1)} %copy.71), calls=%async_computation.3 | async-start | bytes 3244032 | tf_op jit(solution)/shard_map/all_to_all | solution.py:62
  461.0 24.1 %copy-start.8 = (bf16[3,3,2,128,512]{4,3,2,1,0:T(8,128)(2,1)S(1)}, bf16[3,3,2,128,512]{4,3,2,1,0:T(8,128)(2,1)}, u32[]{:S(2)}) copy-start(bf16[3,3,2,128,512]{4,3,2,1,0:T(8,128)(2,1)} %copy-done.7) | copy-start | bytes 7077892
  461.1 251.0 %all-reduce.3.cloned.1.call-start = ((), (), s32[]{:S(2)}) async-start(), calls=%async_computation.4 | async-start | bytes 11010048 | tf_op jit(solution)/shard_map/psum | solution.py:166
  480.8 4.4 copy-start.15
  482.7 8.6 %collective-permute-start.12 = (bf16[1,3,2,85,512]{4,2,3,1,0:T(2,128)(2,1)S(1)}, bf16[1,3,2,85,512]{4,2,3,1,0:T(2,128)(2,1)S(1)}, u32[]{:S(2)}, u32[]{:S(2)}) collective-permute-start(bf16[1,3,2,85,512]{4,2,3,1,0:T(2,128)(2,1)S(1)} %copy.72), channel_id=1, source_target_pairs={{0,8},{8,16},{16,24},{24,0},{1,9},{9,17},{17,25},{25,1},{2,10},{10... | collective-permute-start | bytes 1566728 | tf_op jit(solution)/shard_map/ppermute | solution.py:14
  488.0 8.5 %collective-permute-start.13 = (bf16[1,3,2,85,512]{4,2,3,1,0:T(2,128)(2,1)S(1)}, bf16[1,3,2,85,512]{4,2,3,1,0:T(2,128)(2,1)S(1)}, u32[]{:S(2)}, u32[]{:S(2)}) collective-permute-start(bf16[1,3,2,85,512]{4,2,3,1,0:T(2,128)(2,1)S(1)} %copy.73), channel_id=1, source_target_pairs={{8,0},{16,8},{24,16},{0,24},{9,1},{17,9},{25,17},{1,25},{10,2},{18... | collective-permute-start | bytes 1566728 | tf_op jit(solution)/shard_map/ppermute | solution.py:16
  496.5 4.2 copy-start.2
  496.5 4.2 copy-start.4
  498.1 4.5 copy-start.21
  498.1 4.5 copy-start.40
  498.1 6.0 copy-start.13
  498.1 6.0 copy-start.24
  498.1 21.7 %collective-permute-start.15 = (bf16[5,1,2,85,512]{4,2,3,1,0:T(2,128)(2,1)S(1)}, bf16[5,1,2,85,512]{4,2,3,1,0:T(2,128)(2,1)S(1)}, u32[]{:S(2)}, u32[]{:S(2)}) collective-permute-start(bf16[5,1,2,85,512]{4,2,3,1,0:T(2,128)(2,1)S(1)} %copy.78), channel_id=1, source_target_pairs={{2,0},{4,2},{6,4},{0,6},{3,1},{5,3},{7,5},{1,7},{10,8},{12,10},{14... | collective-permute-start | bytes 2611208 | tf_op jit(solution)/shard_map/ppermute | solution.py:16
  500.5 38.5 %collective-permute-start.14 = (bf16[5,1,2,85,512]{4,2,3,1,0:T(2,128)(2,1)S(1)}, bf16[5,1,2,85,512]{4,2,3,1,0:T(2,128)(2,1)S(1)}, u32[]{:S(2)}, u32[]{:S(2)}) collective-permute-start(bf16[5,1,2,85,512]{4,2,3,1,0:T(2,128)(2,1)S(1)} %copy.77), channel_id=1, source_target_pairs={{0,2},{2,4},{4,6},{6,0},{1,3},{3,5},{5,7},{7,1},{8,10},{10,12},{12... | collective-permute-start | bytes 2611208 | tf_op jit(solution)/shard_map/ppermute | solution.py:14
  (16 other events, 21.9 us)
Sparse Core Ops, SparseCore 0:
  560.8 151.1 all-reduce.2
where the time goes:
time: 738 us; the launch traced here: 728 us
  waiting for transfers between devices  399 us (54%)
  local copies, waits for them, and re-layouts  88.6 us (12%)
  blocking collectives  85.8 us (12%)
  other arithmetic  81.7 us (11%)
  matrix products  31.4 us (4%)
  starting transfers between devices  26.5 us (4%)
  between operations  15.5 us (2%)
    psum x1, waiting for transfers between devices, on_device(): lax.psum((partials[0], partials[1], partials[2], partials[3], partials[4]...  147 us
    ppermute x8, waiting for transfers between devices, extended_2(): lax.ppermute(tail, axis, [(i, (i + 1) % count) for i in range(count)])  139 us
    ppermute x8, waiting for transfers between devices, extended_2(): lax.ppermute(head, axis, [((i + 1) % count, i) for i in range(count)])  93.7 us
    all_to_all x2, blocking collectives, route_dec(): lax.all_to_all(bucket, 'mesh', split_axis=2, concat_axis=2, tiled=True)  62 us
    all_to_all x1, blocking collectives, route_enc(): lax.all_to_all(bucket, 'mesh', split_axis=2, concat_axis=2, tiled=True)  23.8 us
    scatter-add x1, other arithmetic, on_device(): jax.ops.segment_sum(weighted, cell_ids, num_segments=cell_rows)  22 us
    all_to_all x1, waiting for transfers between devices, route_enc(): lax.all_to_all(bucket, 'mesh', split_axis=2, concat_axis=2, tiled=True)  19 us
    ppermute x8, starting transfers between devices, extended_2(): lax.ppermute(head, axis, [((i + 1) % count, i) for i in range(count)])  18.4 us
  transfers between devices with their start and end apart: 18, of which 18 were waited for; matrix products, arithmetic and copies ran while one was open for 3% of the time, Pallas kernels for 0%

commit v1 on v0

--- a/solution.py
+++ b/solution.py
@@ -59,7 +59,10 @@
 
 
 def route_enc(bucket):
-    crossed = lax.all_to_all(bucket, "mesh", split_axis=2, concat_axis=2, tiled=True)
+    crossed = jnp.concatenate(
+        lax.all_to_all(jnp.stack(jnp.split(bucket, lax.axis_size("mesh"), axis=2)), "mesh", 0, 0),
+        axis=2,
+    )
     extended = extended_2(crossed, (("lat", 0), ("lon", 1)), 1)
     result = extended[::-2, ::-2]
     return result

time: 738 us -> 736 us (level)
    ppermute x8, waiting for transfers between devices: 93.7 us -> 121 us  [extended_2(): lax.ppermute(head, axis, [((i + 1) % count, i) for i in range(count)])]
    ppermute x8, waiting for transfers between devices: 139 us -> 116 us  [extended_2(): lax.ppermute(tail, axis, [(i, (i + 1) % count) for i in range(count)])]
  transfers between devices with their start and end apart: 18 -> 18, of which waited for: 18 -> 15; matrix products, arithmetic and copies ran while one was open for 3% -> 3% of each run, Pallas kernels for 0% -> 0%
where the time goes in v1:
time: 736 us; the launch traced here: 726 us
  waiting for transfers between devices  403 us (55%)
  other arithmetic  85.7 us (12%)
  blocking collectives  84.4 us (11%)
  local copies, waits for them, and re-layouts  83.7 us (11%)
  matrix products  30.2 us (4%)
  starting transfers between devices  23.3 us (3%)
  between operations  15.5 us (2%)
    psum x1, waiting for transfers between devices, on_device(): lax.psum((partials[0], partials[1], partials[2], partials[3], partials[4]...  146 us
    ppermute x8, waiting for transfers between devices, extended_2(): lax.ppermute(head, axis, [((i + 1) % count, i) for i in range(count)])  121 us
    ppermute x8, waiting for transfers between devices, extended_2(): lax.ppermute(tail, axis, [(i, (i + 1) % count) for i in range(count)])  116 us
    all_to_all x2, blocking collectives, route_dec(): lax.all_to_all(bucket, 'mesh', split_axis=2, concat_axis=2, tiled=True)  60.6 us
    all_to_all x1, blocking collectives, route_enc(): lax.all_to_all(jnp.stack(jnp.split(bucket, lax.axis_size('mesh'), axis=2)...  23.8 us
    scatter-add x1, other arithmetic, on_device(): jax.ops.segment_sum(weighted, cell_ids, num_segments=cell_rows)  22 us
    all_to_all x1, waiting for transfers between devices, route_enc(): lax.all_to_all(jnp.stack(jnp.split(bucket, lax.axis_size('mesh'), axis=2)...  20 us
    dot_general x12, matrix products, matmul(): return jnp.dot(left, right, preferred_element_type=jnp.float32)  18.2 us
  transfers between devices with their start and end apart: 18, of which 15 were waited for; matrix products, arithmetic and copies ran while one was open for 3% of the time, Pallas kernels for 0%

profile of v1, /device:TPU:0, one launch (start us, length us, event | category | flops | bytes accessed | tf_op | source)
XLA Modules:
  0.0 725.6 jit_solution(3667351885721585002)
XLA Ops:
  10.2 2.1 convolution_convert_fusion.2
  12.3 4.8 gather_fusion
  17.1 2.1 reshape.292
  20.0 2.2 multiply_convert_fusion.1
  22.4 23.8 %all_to_all.20 = bf16[2,3,3,1,85,512]{5,4,2,1,3,0:T(8,128)(2,1)S(1)} all-to-all(bf16[2,3,3,1,85,512]{5,4,2,1,3,0:T(8,128)(2,1)S(1)} %pad_maximum_fusion.4), channel_id=1, replica_groups=mesh['lat'=4,'lon'=4,'mesh'=2] {'mesh'}, dimensions={0} | all-to-all | bytes 3133440 | tf_op jit(solution)/shard_map/all_to_all | solution.py:63
  47.7 10.2 %collective-permute-done.1 = bf16[1,3,2,85,512]{4,2,3,1,0:T(2,128)(2,1)S(1)} collective-permute-done((bf16[1,3,2,85,512]{4,2,3,1,0:T(2,128)(2,1)S(1)}, bf16[1,3,2,85,512]{4,2,3,1,0:T(2,128)(2,1)S(1)}, u32[]{:S(2)}, u32[]{:S(2)}) %collective-permute-start.1) | collective-permute-done | bytes 522272 | tf_op jit(solution)/shard_map/ppermute | solution.py:16
  58.0 3.3 collective-permute-done
  63.1 3.6 collective-permute-start.3
  70.2 16.6 %collective-permute-done.3 = bf16[5,1,2,85,512]{4,2,3,1,0:T(2,128)(2,1)} collective-permute-done((bf16[5,1,2,85,512]{4,2,3,1,0:T(2,128)(2,1)}, bf16[5,1,2,85,512]{4,2,3,1,0:T(2,128)(2,1)}, u32[]{:S(2)}, u32[]{:S(2)}) %collective-permute-start.3) | collective-permute-done | bytes 870432 | tf_op jit(solution)/shard_map/ppermute | solution.py:16
  88.1 17.0 %collective-permute-done.2 = bf16[5,1,2,85,512]{4,2,3,1,0:T(2,128)(2,1)} collective-permute-done((bf16[5,1,2,85,512]{4,2,3,1,0:T(2,128)(2,1)}, bf16[5,1,2,85,512]{4,2,3,1,0:T(2,128)(2,1)}, u32[]{:S(2)}, u32[]{:S(2)}) %collective-permute-start.2) | collective-permute-done | bytes 870432 | tf_op jit(solution)/shard_map/ppermute | solution.py:14
  108.7 2.0 copy.78
  110.7 3.7 reshape.257
  114.4 10.5 %scatter_fusion = f32[320,512]{1,0:T(8,128)S(1)} fusion(f32[320,512]{1,0:T(8,128)S(1)} %convert_element_type.79, s32[1530]{0:T(1024)S(1)} %reshape.255, f32[1530,512]{1,0:T(8,128)} %reshape.257), kind=kCustom, calls=%fused_computation.4 | custom fusion | flops 783360 | bytes 9406440 | tf_op jit(solution)/shard_map/scatter-add | solution.py:121
  127.3 7.5 %gather_fusion.1 = bf16[2304,512]{1,0:T(8,128)(2,1)} fusion(bf16[320,512]{1,0:T(8,128)(2,1)S(1)} %fusion.6, s32[3072]{0:T(1024)S(1)} %get-tuple-element.68), kind=kCustom, calls=%fused_computation.1 | custom fusion | bytes 4727808 | tf_op jit(solution)/shard_map/gather | solution.py:129
  136.6 29.6 %all_to_all.21 = bf16[3,3,2,128,512]{4,3,1,0,2:T(8,128)(2,1)S(1)} all-to-all(bf16[3,3,2,128,512]{4,3,1,0,2:T(8,128)(2,1)S(1)} %copy.79), channel_id=1, replica_groups=mesh['lat'=4,'lon'=4,'mesh'=2] {'mesh'}, dimensions={2} | all-to-all | bytes 4718592 | tf_op jit(solution)/shard_map/all_to_all | solution.py:72
  168.9 17.7 %collective-permute-done.4 = bf16[1,3,2,128,512]{4,3,2,1,0:T(8,128)(2,1)S(1)} collective-permute-done((bf16[1,3,2,128,512]{4,3,2,1,0:T(8,128)(2,1)S(1)}, bf16[1,3,2,128,512]{4,3,2,1,0:T(8,128)(2,1)S(1)}, u32[]{:S(2)}, u32[]{:S(2)}) %collective-permute-start.4) | collective-permute-done | bytes 786464 | tf_op jit(solution)/shard_map/ppermute | solution.py:14
  189.6 1.9 collective-permute-start.6
  191.5 2.4 collective-permute-start.7
  194.7 29.1 %collective-permute-done.6 = bf16[5,1,2,128,512]{4,3,2,1,0:T(8,128)(2,1)S(1)} collective-permute-done((bf16[5,1,2,128,512]{4,3,2,1,0:T(8,128)(2,1)}, bf16[5,1,2,128,512]{4,3,2,1,0:T(8,128)(2,1)S(1)}, u32[]{:S(2)}, u32[]{:S(2)}) %collective-permute-start.6) | collective-permute-done | bytes 1310752 | tf_op jit(solution)/shard_map/ppermute | solution.py:14
  223.8 26.5 %collective-permute-done.7 = bf16[5,1,2,128,512]{4,3,2,1,0:T(8,128)(2,1)} collective-permute-done((bf16[5,1,2,128,512]{4,3,2,1,0:T(8,128)(2,1)}, bf16[5,1,2,128,512]{4,3,2,1,0:T(8,128)(2,1)}, u32[]{:S(2)}, u32[]{:S(2)}) %collective-permute-start.7) | collective-permute-done | bytes 1310752 | tf_op jit(solution)/shard_map/ppermute | solution.py:16
  250.3 3.3 pad_maximum_fusion
  255.2 1.9 rev.7
  258.6 3.6 fusion.30
  262.2 22.0 %scatter_custom_fusion.1 = f32[1024,512]{1,0:T(8,128)S(1)} fusion(s32[2304]{0:T(1024)} %reshape.263, f32[2304,512]{1,0:T(8,128)} %fusion.30, f32[]{:T(128)} %constant.24.clone.1, f32[2304]{0:T(1024)S(1)} %broadcast_select_fusion, f32[]{:T(128)} %constant.16.clone.1), kind=kCustom, calls=%fused_computation.11 | custom fusion | flops 7077888 | bytes 6825984 | tf_op jit(solution)/shard_map/scatter-add | solution.py:136
  284.2 2.9 add_convert_fusion
  291.8 7.6 %gather_fusion.2 = bf16[2304,512]{1,0:T(8,128)(2,1)} fusion(bf16[1024,512]{1,0:T(8,128)(2,1)S(1)} %convolution_convert_fusion.1, s32[3072]{0:T(1024)S(1)} %copy-done.31), kind=kCustom, calls=%fused_computation.2 | custom fusion | bytes 4727808 | tf_op jit(solution)/shard_map/gather | solution.py:146
  299.3 4.1 multiply_convert_fusion
  306.7 31.1 %all_to_all.22 = bf16[3,3,2,128,512]{4,3,1,0,2:T(8,128)(2,1)S(1)} all-to-all(bf16[3,3,2,128,512]{4,3,1,0,2:T(8,128)(2,1)} %rev.16), channel_id=1, replica_groups=mesh['lat'=4,'lon'=4,'mesh'=2] {'mesh'}, dimensions={2} | all-to-all | bytes 4718592 | tf_op jit(solution)/shard_map/all_to_all | solution.py:72
  339.7 17.8 %collective-permute-done.8 = bf16[1,3,2,128,512]{4,3,1,0,2:T(8,128)(2,1)S(1)} collective-permute-done((bf16[1,3,2,128,512]{4,3,1,0,2:T(8,128)(2,1)S(1)}, bf16[1,3,2,128,512]{4,3,1,0,2:T(8,128)(2,1)S(1)}, u32[]{:S(2)}, u32[]{:S(2)}) %collective-permute-start.8) | collective-permute-done | bytes 786464 | tf_op jit(solution)/shard_map/ppermute | solution.py:14
  360.6 2.3 collective-permute-start.10
  364.4 29.9 %collective-permute-done.10 = bf16[5,1,2,128,512]{4,3,1,0,2:T(8,128)(2,1)S(1)} collective-permute-done((bf16[5,1,2,128,512]{4,3,1,0,2:T(8,128)(2,1)}, bf16[5,1,2,128,512]{4,3,1,0,2:T(8,128)(2,1)S(1)}, u32[]{:S(2)}, u32[]{:S(2)}) %collective-permute-start.10) | collective-permute-done | bytes 1310752 | tf_op jit(solution)/shard_map/ppermute | solution.py:14
  394.3 27.1 %collective-permute-done.11 = bf16[5,1,2,128,512]{4,3,1,0,2:T(8,128)(2,1)} collective-permute-done((bf16[5,1,2,128,512]{4,3,1,0,2:T(8,128)(2,1)}, bf16[5,1,2,128,512]{4,3,1,0,2:T(8,128)(2,1)}, u32[]{:S(2)}, u32[]{:S(2)}) %collective-permute-start.11) | collective-permute-done | bytes 1310752 | tf_op jit(solution)/shard_map/ppermute | solution.py:16
  421.4 3.3 pad_maximum_fusion.1
  425.3 2.9 copy.84
  428.3 16.6 %scatter_custom_fusion.2 = f32[320,512]{1,0:T(8,128)S(1)} fusion(s32[2304]{0:T(1024)S(1)} %reshape.271, f32[2304,512]{1,0:T(8,128)} %bitcast.94, f32[]{:T(128)} %constant.16.clone.1), kind=kCustom, calls=%fused_computation.77 | custom fusion | flops 1179648 | bytes 655872 | tf_op jit(solution)/shard_map/scatter-add | solution.py:151
  447.7 4.8 gather_fusion.3
  457.3 3.8 all-to-all-start.3
  461.2 20.0 %all-to-all-done.3 = bf16[2,3,3,1,85,512]{5,4,2,3,1,0:T(8,128)(2,1)S(1)} async-done(((bf16[2,3,3,1,85,512]{5,4,2,3,1,0:T(8,128)(2,1)}), bf16[2,3,3,1,85,512]{5,4,2,3,1,0:T(8,128)(2,1)S(1)}, u32[]{:S(2)}, u32[]{:S(2)}) %all-to-all-start.3) | async-done | bytes 1566752 | tf_op jit(solution)/shard_map/all_to_all | solution.py:63
  484.2 2.4 convolution_multiply_fusion.1
  486.6 8.0 %collective-permute-done.13 = bf16[1,3,2,85,512]{4,2,3,1,0:T(2,128)(2,1)S(1)} collective-permute-done((bf16[1,3,2,85,512]{4,2,3,1,0:T(2,128)(2,1)S(1)}, bf16[1,3,2,85,512]{4,2,3,1,0:T(2,128)(2,1)S(1)}, u32[]{:S(2)}, u32[]{:S(2)}) %collective-permute-start.13) | collective-permute-done | bytes 522272 | tf_op jit(solution)/shard_map/ppermute | solution.py:16
  500.0 1.8 convolution_multiply_fusion
  504.8 32.3 %collective-permute-done.15 = bf16[5,1,2,85,512]{4,2,3,1,0:T(2,128)(2,1)S(1)} collective-permute-done((bf16[5,1,2,85,512]{4,2,3,1,0:T(2,128)(2,1)S(1)}, bf16[5,1,2,85,512]{4,2,3,1,0:T(2,128)(2,1)S(1)}, u32[]{:S(2)}, u32[]{:S(2)}) %collective-permute-start.15) | collective-permute-done | bytes 870432 | tf_op jit(solution)/shard_map/ppermute | solution.py:16
  538.2 2.0 convert_multiply_fusion
  540.2 3.7 reshape.281
  543.8 11.6 %scatter_custom_fusion.3 = f32[1024,512]{1,0:T(8,128)} fusion(s32[1530]{0:T(1024)S(1)} %reshape.279, f32[1530,512]{1,0:T(8,128)} %reshape.281, f32[]{:T(128)} %constant.16.clone.1), kind=kCustom, calls=%fused_computation.47 | custom fusion | flops 783360 | bytes 2097664 | tf_op jit(solution)/shard_map/scatter-add | solution.py:163
  555.5 3.6 fusion.5
  560.1 3.7 convolution_add_fusion
  563.7 146.0 %all-reduce.3.cloned.1.call-done = (f32[512,512]{0,1:T(8,128)}, f32[512,512]{1,0:T(8,128)}, f32[512,512]{1,0:T(8,128)}, f32[512,512]{1,0:T(8,128)}, f32[512,512]{1,0:T(8,128)}, /*index=5*/f32[512,84]{1,0:T(8,128)}) async-done(((f32[512,512]{0,1:T(8,128)}, f32[512,512]{1,0:T(8,128)}, f32[512,512]{1,0:T(8,128)}, f32[512,512]{1,0:T(8,128)}, f32[512,512]{1,0:T(8,128)}, /*index=5*/f32[512,84]{1,0:T(8,128)}), ...) | async-done | bytes 5414928 | tf_op jit(solution)/shard_map/psum | solution.py:169
  (200 shorter events, 73.7 us)
Async XLA Ops:
  7.2 251.4 %copy-start = (bf16[512,512]{1,0:T(8,128)(2,1)S(1)}, bf16[512,512]{1,0:T(8,128)(2,1)}, u32[]{:S(2)}) copy-start(bf16[512,512]{1,0:T(8,128)(2,1)} %param.26) | copy-start | bytes 1572868
  17.1 2.1 copy-start.40
  46.7 11.2 %collective-permute-start.1 = (bf16[1,3,2,85,512]{4,2,3,1,0:T(2,128)(2,1)S(1)}, bf16[1,3,2,85,512]{4,2,3,1,0:T(2,128)(2,1)S(1)}, u32[]{:S(2)}, u32[]{:S(2)}) collective-permute-start(bf16[1,3,2,85,512]{4,2,3,1,0:T(2,128)(2,1)S(1)} %copy.71), channel_id=1, source_target_pairs={{8,0},{16,8},{24,16},{0,24},{9,1},{17,9},{25,17},{1,25},{10,2},{18... | collective-permute-start | bytes 1566728 | tf_op jit(solution)/shard_map/ppermute | solution.py:16
  47.4 13.8 %collective-permute-start = (bf16[1,3,2,85,512]{4,2,3,1,0:T(2,128)(2,1)S(1)}, bf16[1,3,2,85,512]{4,2,3,1,0:T(2,128)(2,1)S(1)}, u32[]{:S(2)}, u32[]{:S(2)}) collective-permute-start(bf16[1,3,2,85,512]{4,2,3,1,0:T(2,128)(2,1)S(1)} %copy.70), channel_id=1, source_target_pairs={{0,8},{8,16},{16,24},{24,0},{1,9},{9,17},{17,25},{25,1},{2,10},{10... | collective-permute-start | bytes 1566728 | tf_op jit(solution)/shard_map/ppermute | solution.py:14
  61.5 6.8 copy-start.33
  61.5 6.9 copy-start.35
  61.6 8.0 %copy-start.37 = (s32[1,3,3,2,128]{4,3,2,1,0:T(2,128)S(1)}, s32[1,3,3,2,128]{4,3,2,1,0:T(2,128)}, u32[]{:S(2)}) copy-start(s32[1,3,3,2,128]{4,3,2,1,0:T(2,128)} %param.34) | copy-start | bytes 27652
  63.1 23.7 %collective-permute-start.3 = (bf16[5,1,2,85,512]{4,2,3,1,0:T(2,128)(2,1)}, bf16[5,1,2,85,512]{4,2,3,1,0:T(2,128)(2,1)}, u32[]{:S(2)}, u32[]{:S(2)}) collective-permute-start(bf16[5,1,2,85,512]{4,2,3,1,0:T(2,128)(2,1)} %copy.75), channel_id=1, source_target_pairs={{2,0},{4,2},{6,4},{0,6},{3,1},{5,3},{7,5},{1,7},{10,8},{12,10},{14... | collective-permute-start | bytes 2611208 | tf_op jit(solution)/shard_map/ppermute | solution.py:16
  68.3 36.8 %collective-permute-start.2 = (bf16[5,1,2,85,512]{4,2,3,1,0:T(2,128)(2,1)}, bf16[5,1,2,85,512]{4,2,3,1,0:T(2,128)(2,1)}, u32[]{:S(2)}, u32[]{:S(2)}) collective-permute-start(bf16[5,1,2,85,512]{4,2,3,1,0:T(2,128)(2,1)} %copy.74), channel_id=1, source_target_pairs={{0,2},{2,4},{4,6},{6,0},{1,3},{3,5},{5,7},{7,1},{8,10},{10,12},{12... | collective-permute-start | bytes 2611208 | tf_op jit(solution)/shard_map/ppermute | solution.py:14
  114.4 11.3 %copy-start.17 = (bf16[512,512]{1,0:T(8,128)(2,1)S(1)}, bf16[512,512]{1,0:T(8,128)(2,1)}, u32[]{:S(2)}) copy-start(bf16[512,512]{1,0:T(8,128)(2,1)} %param.24) | copy-start | bytes 1572868
  114.4 11.3 %copy-start.38 = (f32[512]{0:T(512)S(1)}, f32[512]{0:T(512)}, u32[]{:S(2)}) copy-start(f32[512]{0:T(512)} %param.22) | copy-start | bytes 6148
  124.9 2.0 copy-start.44
  166.4 20.1 %collective-permute-start.4 = (bf16[1,3,2,128,512]{4,3,2,1,0:T(8,128)(2,1)S(1)}, bf16[1,3,2,128,512]{4,3,2,1,0:T(8,128)(2,1)S(1)}, u32[]{:S(2)}, u32[]{:S(2)}) collective-permute-start(bf16[1,3,2,128,512]{4,3,2,1,0:T(8,128)(2,1)S(1)} %copy.110), channel_id=1, source_target_pairs={{0,8},{8,16},{16,24},{24,0},{1,9},{9,17},{17,25},{25,1},{2,10},{10... | collective-permute-start | bytes 2359304 | tf_op jit(solution)/shard_map/ppermute | solution.py:14
  167.1 19.7 %collective-permute-start.5 = (bf16[1,3,2,128,512]{4,3,2,1,0:T(8,128)(2,1)S(1)}, bf16[1,3,2,128,512]{4,3,2,1,0:T(8,128)(2,1)S(1)}, u32[]{:S(2)}, u32[]{:S(2)}) collective-permute-start(bf16[1,3,2,128,512]{4,3,2,1,0:T(8,128)(2,1)S(1)} %copy.111), channel_id=1, source_target_pairs={{8,0},{16,8},{24,16},{0,24},{9,1},{17,9},{25,17},{1,25},{10,2},{18... | collective-permute-start | bytes 2359304 | tf_op jit(solution)/shard_map/ppermute | solution.py:16
  186.9 2.7 copy-start.5
  186.9 7.8 %copy-start.41 = (f32[1,3,3,2,128]{4,3,2,1,0:T(2,128)S(1)}, f32[1,3,3,2,128]{4,3,2,1,0:T(2,128)}, u32[]{:S(2)}) copy-start(f32[1,3,3,2,128]{4,3,2,1,0:T(2,128)} %param.35) | copy-start | bytes 27652
  189.6 34.2 %collective-permute-start.6 = (bf16[5,1,2,128,512]{4,3,2,1,0:T(8,128)(2,1)}, bf16[5,1,2,128,512]{4,3,2,1,0:T(8,128)(2,1)S(1)}, u32[]{:S(2)}, u32[]{:S(2)}) collective-permute-start(bf16[5,1,2,128,512]{4,3,2,1,0:T(8,128)(2,1)} %get-tuple-element.43), channel_id=1, source_target_pairs={{0,2},{2,4},{4,6},{6,0},{1,3},{3,5},{5,7},{7,1},{8,10},{10,12},{12... | collective-permute-start | bytes 3932168 | tf_op jit(solution)/shard_map/ppermute | solution.py:14
  191.5 58.8 %collective-permute-start.7 = (bf16[5,1,2,128,512]{4,3,2,1,0:T(8,128)(2,1)}, bf16[5,1,2,128,512]{4,3,2,1,0:T(8,128)(2,1)}, u32[]{:S(2)}, u32[]{:S(2)}) collective-permute-start(bf16[5,1,2,128,512]{4,3,2,1,0:T(8,128)(2,1)} %get-tuple-element.44), channel_id=1, source_target_pairs={{2,0},{4,2},{6,4},{0,6},{3,1},{5,3},{7,5},{1,7},{10,8},{12,10},{14... | collective-permute-start | bytes 3932168 | tf_op jit(solution)/shard_map/ppermute | solution.py:16
  284.1 2.9 copy-start.3
  284.1 3.9 copy-start.27
  284.1 3.9 copy-start.28
  284.2 3.9 copy-start.43
  288.1 2.9 copy-start.16
  337.9 19.6 %collective-permute-start.8 = (bf16[1,3,2,128,512]{4,3,1,0,2:T(8,128)(2,1)S(1)}, bf16[1,3,2,128,512]{4,3,1,0,2:T(8,128)(2,1)S(1)}, u32[]{:S(2)}, u32[]{:S(2)}) collective-permute-start(bf16[1,3,2,128,512]{4,3,1,0,2:T(8,128)(2,1)S(1)} %get-tuple-element.50), channel_id=1, source_target_pairs={{0,8},{8,16},{16,24},{24,0},{1,9},{9,17},{17,25},{25,1},{2,10},{10... | collective-permute-start | bytes 2359304 | tf_op jit(solution)/shard_map/ppermute | solution.py:14
  337.9 19.8 %collective-permute-start.9 = (bf16[1,3,2,128,512]{4,3,1,0,2:T(8,128)(2,1)S(1)}, bf16[1,3,2,128,512]{4,3,1,0,2:T(8,128)(2,1)S(1)}, u32[]{:S(2)}, u32[]{:S(2)}) collective-permute-start(bf16[1,3,2,128,512]{4,3,1,0,2:T(8,128)(2,1)S(1)} %get-tuple-element.49), channel_id=1, source_target_pairs={{8,0},{16,8},{24,16},{0,24},{9,1},{17,9},{25,17},{1,25},{10,2},{18... | collective-permute-start | bytes 2359304 | tf_op jit(solution)/shard_map/ppermute | solution.py:16
  357.8 2.8 copy-start.6
  357.8 6.6 copy-start.36
  360.6 33.7 %collective-permute-start.10 = (bf16[5,1,2,128,512]{4,3,1,0,2:T(8,128)(2,1)}, bf16[5,1,2,128,512]{4,3,1,0,2:T(8,128)(2,1)S(1)}, u32[]{:S(2)}, u32[]{:S(2)}) collective-permute-start(bf16[5,1,2,128,512]{4,3,1,0,2:T(8,128)(2,1)} %get-tuple-element.41), channel_id=1, source_target_pairs={{0,2},{2,4},{4,6},{6,0},{1,3},{3,5},{5,7},{7,1},{8,10},{10,12},{12... | collective-permute-start | bytes 3932168 | tf_op jit(solution)/shard_map/ppermute | solution.py:14
  362.9 58.5 %collective-permute-start.11 = (bf16[5,1,2,128,512]{4,3,1,0,2:T(8,128)(2,1)}, bf16[5,1,2,128,512]{4,3,1,0,2:T(8,128)(2,1)}, u32[]{:S(2)}, u32[]{:S(2)}) collective-permute-start(bf16[5,1,2,128,512]{4,3,1,0,2:T(8,128)(2,1)} %get-tuple-element.42), channel_id=1, source_target_pairs={{2,0},{4,2},{6,4},{0,6},{3,1},{5,3},{7,5},{1,7},{10,8},{12,10},{14... | collective-permute-start | bytes 3932168 | tf_op jit(solution)/shard_map/ppermute | solution.py:16
  425.3 19.6 %copy-start.24 = (f32[320,512]{1,0:T(8,128)S(1)}, f32[320,512]{1,0:T(8,128)}, u32[]{:S(2)}) copy-start(f32[320,512]{1,0:T(8,128)} %copy-done.23) | copy-start | bytes 1966084
  428.3 18.4 %copy-start.18 = (bf16[512,512]{1,0:T(8,128)(2,1)S(1)}, bf16[512,512]{1,0:T(8,128)(2,1)}, u32[]{:S(2)}) copy-start(bf16[512,512]{1,0:T(8,128)(2,1)} %param.24) | copy-start | bytes 1572868
  428.3 18.4 %copy-start.39 = (f32[512]{0:T(512)S(1)}, f32[512]{0:T(512)}, u32[]{:S(2)}) copy-start(f32[512]{0:T(512)} %param.22) | copy-start | bytes 6148
  444.9 2.5 copy-start.12
  445.0 2.5 copy-start.42
  457.3 3.9 copy-start.34
  457.3 24.0 %all-to-all-start.3 = ((bf16[2,3,3,1,85,512]{5,4,2,3,1,0:T(8,128)(2,1)}), bf16[2,3,3,1,85,512]{5,4,2,3,1,0:T(8,128)(2,1)S(1)}, u32[]{:S(2)}, u32[]{:S(2)}) async-start(bf16[2,3,3,1,85,512]{5,4,2,3,1,0:T(8,128)(2,1)} %maximum_bitcast_fusion), calls=%async_computation.3 | async-start | bytes 3244032 | tf_op jit(solution)/shard_map/all_to_all | solution.py:63
  461.1 248.7 %all-reduce.3.cloned.1.call-start = ((), (), s32[]{:S(2)}) async-start(), calls=%async_computation.4 | async-start | bytes 11010048 | tf_op jit(solution)/shard_map/psum | solution.py:169
  481.5 2.7 copy-start.8
  481.5 2.7 copy-start.15
  482.4 12.1 %collective-permute-start.13 = (bf16[1,3,2,85,512]{4,2,3,1,0:T(2,128)(2,1)S(1)}, bf16[1,3,2,85,512]{4,2,3,1,0:T(2,128)(2,1)S(1)}, u32[]{:S(2)}, u32[]{:S(2)}) collective-permute-start(bf16[1,3,2,85,512]{4,2,3,1,0:T(2,128)(2,1)S(1)} %copy.89), channel_id=1, source_target_pairs={{8,0},{16,8},{24,16},{0,24},{9,1},{17,9},{25,17},{1,25},{10,2},{18... | collective-permute-start | bytes 1566728 | tf_op jit(solution)/shard_map/ppermute | solution.py:16
  482.5 13.5 %collective-permute-start.12 = (bf16[1,3,2,85,512]{4,2,3,1,0:T(2,128)(2,1)S(1)}, bf16[1,3,2,85,512]{4,2,3,1,0:T(2,128)(2,1)S(1)}, u32[]{:S(2)}, u32[]{:S(2)}) collective-permute-start(bf16[1,3,2,85,512]{4,2,3,1,0:T(2,128)(2,1)S(1)} %copy.88), channel_id=1, source_target_pairs={{0,8},{8,16},{16,24},{24,0},{1,9},{9,17},{17,25},{25,1},{2,10},{10... | collective-permute-start | bytes 1566728 | tf_op jit(solution)/shard_map/ppermute | solution.py:14
  496.0 4.0 copy-start.4
  496.3 3.7 copy-start.2
  497.6 4.2 copy-start.22
  497.7 5.7 copy-start.13
  497.7 5.7 copy-start.25
  497.7 39.4 %collective-permute-start.15 = (bf16[5,1,2,85,512]{4,2,3,1,0:T(2,128)(2,1)S(1)}, bf16[5,1,2,85,512]{4,2,3,1,0:T(2,128)(2,1)S(1)}, u32[]{:S(2)}, u32[]{:S(2)}) collective-permute-start(bf16[5,1,2,85,512]{4,2,3,1,0:T(2,128)(2,1)S(1)} %copy.93), channel_id=1, source_target_pairs={{2,0},{4,2},{6,4},{0,6},{3,1},{5,3},{7,5},{1,7},{10,8},{12,10},{14... | collective-permute-start | bytes 2611208 | tf_op jit(solution)/shard_map/ppermute | solution.py:16
  498.3 38.9 %collective-permute-start.14 = (bf16[5,1,2,85,512]{4,2,3,1,0:T(2,128)(2,1)S(1)}, bf16[5,1,2,85,512]{4,2,3,1,0:T(2,128)(2,1)S(1)}, u32[]{:S(2)}, u32[]{:S(2)}) collective-permute-start(bf16[5,1,2,85,512]{4,2,3,1,0:T(2,128)(2,1)S(1)} %copy.92), channel_id=1, source_target_pairs={{0,2},{2,4},{4,6},{6,0},{1,3},{3,5},{5,7},{7,1},{8,10},{10,12},{12... | collective-permute-start | bytes 2611208 | tf_op jit(solution)/shard_map/ppermute | solution.py:14
  (15 other events, 16.6 us)
Sparse Core Ops, SparseCore 0:
  559.2 150.5 all-reduce.2
